TPU v7x, 32 devices: a whole 2x2x4 slice. The times are simulated.
32 devices in a mesh: seq: 16 (over z, y, x), head: 2 (over core).
Axes of the slice: x: 2, y: 2, z: 4, core: 2. Of those that a mesh axis runs over, the one named last changes fastest.
Arguments:
- tokens: bfloat16 [16, 1024, 3072], P('seq', None, 'head'), may hold values from -6 to 6
- fast_state: float32 [16, 8, 192, 2304], P('seq', 'head'), may hold values from -6 to 6
- momentum: float32 [16, 8, 192, 2304], P('seq', 'head'), may hold values from -1.8 to 1.8
- init_fast: bfloat16 [8, 192, 2304], P('head'), may hold values from -6 to 6
- past_keys: bfloat16 [16, 2048, 1536], P('seq', None, 'head'), may hold values from -6 to 6
- past_values: bfloat16 [16, 2048, 1536], P('seq', None, 'head'), may hold values from -6 to 6
- qkv_weight: bfloat16 [3, 3072, 1536], P(None, 'seq', 'head'), may hold values from -0.109375 to 0.109375
- rate_weight: bfloat16 [3072, 8], P(None, 'head'), may hold values from -0.109375 to 0.109375
- out_weight: bfloat16 [1536, 3072], P('head'), may hold values from -0.15625 to 0.15625
- prompt_begins: int32 [2, 16], replicated, may hold values 0 or 1
Outputs:
- mixed: bfloat16 [16, 1024, 3072], P('seq', None, 'head')
- fast_out: float32 [16, 8, 192, 2304], P('seq', 'head')
- momentum_out: float32 [16, 8, 192, 2304], P('seq', 'head')
All inputs are finite; a program needn't handle non-finite values.
Results may differ from a plain program's by a relative error of at most 0.015.
Values may be sent and summed in bfloat16 or wider, within the bound.
A program may use at most 192 MiB of HBM per device.

v0:
```python
import math
import jax
import jax.numpy as jnp
from jax import lax
from jax.sharding import PartitionSpec as P

SPAN = 512
WINDOW = 2048
STEPS = 2
momentum_decay = 0.9
rate_scale = 0.3
epsilon = 1e-06
highest = lax.Precision.HIGHEST


def passed_along(block, axis, distance):
    devices = range(lax.axis_size(axis))
    route = [((i - distance) % len(devices), i) for i in devices]
    return lax.ppermute(block, axis, route)


def unit_rows(matrix):
    return matrix * lax.rsqrt(jnp.mean(matrix * matrix, axis=-1, keepdims=True) + epsilon)


def head_span(
    queries,
    keys_span,
    values_span,
    step_size,
    window_keys,
    window_values,
    visible_prev,
    restart,
    weights_now,
    momentum_now,
    initial,
):
    span_len = queries.shape[0]
    window_len = window_keys.shape[0]
    head_dim = queries.shape[1]
    hidden = weights_now.shape[1] // 3
    score_bound = math.sqrt(head_dim)
    query_unit = unit_rows(queries.astype(jnp.float32))
    key_unit = unit_rows(keys_span.astype(jnp.float32))
    context_keys = jnp.concatenate(
        [unit_rows(window_keys.astype(jnp.float32)), key_unit], axis=0
    ).astype(jnp.bfloat16)
    context_values = jnp.concatenate([window_values, values_span], axis=0)
    scores = (
        lax.dot_general(
            query_unit.astype(jnp.bfloat16),
            context_keys,
            (((1,), (1,)), ((), ())),
            preferred_element_type=jnp.float32,
        )
        / score_bound
    )
    query_pos = lax.broadcasted_iota(jnp.int32, scores.shape, 0)
    key_pos = lax.broadcasted_iota(jnp.int32, scores.shape, 1)
    restart_flag = restart.astype(jnp.float32)
    keep_prev = jnp.concatenate(
        [visible_prev * (1.0 - restart_flag), jnp.ones((span_len,), jnp.float32)]
    )
    inside = (key_pos > query_pos) & (key_pos <= query_pos + window_len)
    soft_weights = jnp.where(inside, jnp.exp(scores - score_bound), 0.0) * keep_prev[None, :]
    denominator = jnp.sum(soft_weights, axis=1, keepdims=True)
    attended = (
        jnp.dot(
            soft_weights.astype(jnp.bfloat16), context_values, preferred_element_type=jnp.float32
        )
        / denominator
    )
    weights_now = jnp.where(restart > 0, initial.astype(jnp.float32), weights_now)
    momentum_now = jnp.where(restart > 0, jnp.zeros_like(momentum_now), momentum_now)
    up_proj = weights_now[:, : 2 * hidden]
    down_proj = weights_now[:, 2 * hidden :]
    hidden_scale = math.sqrt(hidden)
    query_in = query_unit / score_bound
    key_in = key_unit / score_bound
    both_in = jnp.dot(query_in, up_proj, precision=highest, preferred_element_type=jnp.float32)
    mixed_hidden = jax.nn.silu(both_in[:, :hidden]) * both_in[:, hidden:]
    applied = (
        lax.dot_general(
            mixed_hidden,
            down_proj,
            (((1,), (1,)), ((), ())),
            precision=highest,
            preferred_element_type=jnp.float32,
        )
        / hidden_scale
    )
    both_key = jnp.dot(key_in, up_proj, precision=highest, preferred_element_type=jnp.float32)
    gate_key = both_key[:, :hidden]
    lift_key = both_key[:, hidden:]
    gate_sigmoid = jax.nn.sigmoid(gate_key)
    gate_silu = gate_key * gate_sigmoid
    hidden_key = gate_silu * lift_key
    out_grad = -step_size.astype(jnp.float32)[:, None] * values_span.astype(jnp.float32)
    down_grad = (
        lax.dot_general(
            out_grad,
            hidden_key,
            (((0,), (0,)), ((), ())),
            precision=highest,
            preferred_element_type=jnp.float32,
        )
        / hidden_scale
    )
    hidden_grad = (
        jnp.dot(out_grad, down_proj, precision=highest, preferred_element_type=jnp.float32)
        / hidden_scale
    )
    gate_grad = hidden_grad * lift_key * gate_sigmoid * (1.0 + gate_key * (1.0 - gate_sigmoid))
    lift_grad = hidden_grad * gate_silu
    up_grad = lax.dot_general(
        key_in,
        jnp.concatenate([gate_grad, lift_grad], axis=1),
        (((0,), (0,)), ((), ())),
        precision=highest,
        preferred_element_type=jnp.float32,
    )
    gradient = jnp.concatenate([up_grad, down_grad], axis=1)
    momentum_new = momentum_decay * momentum_now + gradient
    stepped = weights_now - momentum_new
    weights_new = stepped * lax.rsqrt(jnp.mean(stepped * stepped, axis=0, keepdims=True) + epsilon)
    head_mix = (attended + applied).astype(jnp.bfloat16)
    return (head_mix, weights_new, momentum_new)


def position_span(
    queries,
    keys_span,
    values_span,
    step_size,
    window_keys,
    window_values,
    visible_prev,
    restart,
    weights_now,
    momentum_now,
    initial,
):
    heads_here = weights_now.shape[0]

    def split_heads(matrix):
        return matrix.reshape(matrix.shape[0], heads_here, matrix.shape[1] // heads_here)

    mapped = jax.vmap(
        head_span, in_axes=(1, 1, 1, 1, 1, 1, None, None, 0, 0, 0), out_axes=(1, 0, 0)
    )
    head_mix, weights_new, momentum_new = mapped(
        split_heads(queries),
        split_heads(keys_span),
        split_heads(values_span),
        step_size,
        split_heads(window_keys),
        split_heads(window_values),
        visible_prev,
        restart,
        weights_now,
        momentum_now,
        initial,
    )
    return (head_mix.reshape(head_mix.shape[0], -1), weights_new, momentum_new)


def next_window(window_keys, window_values, visible_prev, restart, keys_span, values_span):
    window_len = window_keys.shape[0]
    kept_rows = visible_prev * (1.0 - restart.astype(visible_prev.dtype))
    fresh_rows = jnp.ones((keys_span.shape[0],), visible_prev.dtype)
    new_keys = jnp.concatenate([window_keys, keys_span], axis=0)[-window_len:]
    new_values = jnp.concatenate([window_values, values_span], axis=0)[-window_len:]
    new_visible = jnp.concatenate([kept_rows, fresh_rows])[-window_len:]
    return (new_keys, new_values, new_visible)


def reduce_section(head_mix, out_weight):
    partial_value = jnp.dot(head_mix, out_weight, preferred_element_type=jnp.float32)
    return lax.psum_scatter(
        partial_value.astype(jnp.bfloat16), "head", scatter_dimension=1, tiled=True
    ).astype(jnp.float32)


def body(
    tokens,
    fast_state,
    momentum,
    init_fast,
    past_keys,
    past_values,
    qkv_weight,
    rate_weight,
    out_weight,
    prompt_begins,
):
    position_index = lax.axis_index("seq")
    features = lax.all_gather(tokens[0], "head", axis=1, tiled=True)
    projected = jnp.einsum(
        "tr,crh->cth",
        features,
        lax.all_gather(qkv_weight, "seq", axis=1, tiled=True),
        preferred_element_type=jnp.float32,
    )
    projected_bf = projected.astype(jnp.bfloat16)
    step_sizes = (
        rate_scale
        * jax.nn.softplus(jnp.dot(features, rate_weight, preferred_element_type=jnp.float32))
    ).astype(jnp.bfloat16)
    weights_now = fast_state[0]
    momentum_now = momentum[0]
    window_keys = past_keys[0]
    window_values = past_values[0]
    visible = jnp.ones((WINDOW,), jnp.float32)
    mix_blocks = []
    reduced_parts = []
    for section_index in range(STEPS):
        first_row = section_index * SPAN
        span_bf = projected_bf[:, first_row : first_row + SPAN]
        span_rates = step_sizes[first_row : first_row + SPAN]
        restart = prompt_begins[section_index, position_index]
        head_mix, weights_new, momentum_new = position_span(
            span_bf[0],
            span_bf[1],
            span_bf[2],
            span_rates,
            window_keys,
            window_values,
            visible,
            restart,
            weights_now,
            momentum_now,
            init_fast,
        )
        window_keys, window_values, visible = next_window(
            window_keys, window_values, visible, restart, span_bf[1], span_bf[2]
        )
        if section_index + 1 < STEPS:
            weights_now, momentum_now = (
                passed_along(weights_new.astype(jnp.bfloat16), "seq", 1).astype(weights_new.dtype),
                passed_along(momentum_new.astype(jnp.bfloat16), "seq", 1).astype(
                    momentum_new.dtype
                ),
            )
            window_keys, window_values, visible_wire = passed_along(
                (window_keys, window_values, visible.astype(jnp.bfloat16)), "seq", 1
            )
            visible = visible_wire.astype(jnp.float32)
        else:
            weights_now = weights_new
            momentum_now = momentum_new
        mix_blocks.append(head_mix)
        reduced_parts.append(reduce_section(head_mix, out_weight))
    mixed = jnp.concatenate(reduced_parts, axis=0)
    return (mixed.astype(jnp.bfloat16)[None], weights_now[None], momentum_now[None])


def solution(mesh):
    in_specs = (
        P("seq", None, "head"),
        P("seq", "head", None, None),
        P("seq", "head", None, None),
        P("head", None, None),
        P("seq", None, "head"),
        P("seq", None, "head"),
        P(None, "seq", "head"),
        P(None, "head"),
        P("head", None),
        P(),
    )
    out_specs = (P("seq", None, "head"), P("seq", "head", None, None), P("seq", "head", None, None))
    return jax.shard_map(body, mesh=mesh, in_specs=in_specs, out_specs=out_specs, check_vma=False)
```

profile of v0, /device:TPU:0, one launch (start us, length us, event | category | flops | bytes accessed | tf_op | source)
XLA Modules:
  0.0 601.0 jit_solution(12368685986231815268)
XLA Ops:
  26.7 6.9 %convert_select_fusion.1 = f32[4,192,2304]{2,1,0:T(8,128)} fusion(bf16[4,192,2304]{2,1,0:T(8,128)(2,1)S(1)} %copy-done.4, f32[1,4,192,2304]{3,2,1,0:T(8,128)} %param.11, pred[]{:T(512)} %bitcast.21), kind=kLoop, calls=%fused_computation.19 | loop fusion | flops 3538944 | bytes 17694720 | tf_op jit(solution)/shard_map/vmap(jit(_where))/select_n | solution.py:74
  46.2 153.0 %all-gather.4.cloned.1.call-done = bf16[3,3072,768]{2,1,0:T(8,128)(2,1)} async-done(((bf16[3,192,768]{2,1,0:T(8,128)(2,1)}), bf16[3,3072,768]{2,1,0:T(8,128)(2,1)}) %all-gather.4.cloned.1.call-update) | async-done | bytes 14155792 | tf_op jit(solution)/shard_map/all_gather | solution.py:202
  199.2 19.5 %convert_bitcast_fusion = bf16[3,1024,768]{1,2,0:T(8,128)(2,1)S(1)} fusion(bf16[3,3072,768]{2,1,0:T(8,128)(2,1)} %all-gather.4.cloned.1.call-done, bf16[1,1024,3072]{2,1,0:T(8,128)(2,1)} %all-gather.6.cloned.1.call-done), kind=kOutput, calls=%fused_computation.67 | convolution fusion | flops 14497873920 | bytes 25165824 | tf_op jit(solution)/shard_map/tr,crh->cth/dot_general | solution.py:199
  220.7 13.2 %fusion.49 = f32[4,512,1536]{2,1,0:T(8,128)S(1)} fusion(f32[4,192,2304]{2,1,0:T(8,128)} %convert_select_fusion.1, bf16[512,4,192]{0,2,1:T(8,128)(2,1)S(1)} %bitcast.160, f32[4,512]{1,0:T(4,128)S(1)} %rsqrt_bitcast_fusion.4), kind=kOutput, calls=%fused_computation.74 | convolution fusion | flops 7248936960 | bytes 18096128 | tf_op jit(solution)/shard_map/vmap()/dot_general | solution.py:93
  233.9 7.3 %fusion.79 = f32[4,192,768]{2,1,0:T(8,128)} fusion(f32[4,512,1536]{2,1,0:T(8,128)S(1)} %fusion.49, bf16[4,512,192]{1,2,0:T(8,128)(2,1)S(1)} %bitcast.178, f32[4,512]{1,0:T(4,128)S(1)} %get-tuple-element.23), kind=kOutput, calls=%fused_computation.113 | convolution fusion | flops 3633119232 | bytes 15736832 | tf_op jit(solution)/shard_map/vmap()/dot_general | solution.py:101
  241.1 13.6 %add_multiply_fusion.1 = (f32[4,512,768]{2,1,0:T(8,128)}, f32[4,512,768]{2,1,0:T(8,128)}) fusion(f32[4,512,1536]{2,1,0:T(8,128)S(1)} %fusion.49, f32[4,192,2304]{2,1,0:T(8,128)} %convert_select_fusion.1, bf16[4,512,192]{1,2,0:T(8,128)(2,1)S(1)} %bitcast.179, f32[4,512]{1,0:T(4,128)S(1)} %get-tuple-element.23), kind=kOutput, calls=%fused_computation.49 | convolution fusion | flops 3643539456 | bytes 28319744 | tf_op jit(solution)/shard_map/vmap()/dot_general | solution.py:111
  267.0 11.5 %fusion.4 = f32[4,192,1536]{2,1,0:T(8,128)S(1)} fusion(f32[4,512,768]{2,1,0:T(8,128)} %get-tuple-element.10, f32[4,512,768]{2,1,0:T(8,128)} %get-tuple-element.9, bf16[512,4,192]{0,2,1:T(8,128)(2,1)S(1)} %bitcast.161, f32[4,512]{1,0:T(4,128)S(1)} %rsqrt_bitcast_fusion.4), kind=kOutput, calls=%fused_computation.6 | convolution fusion | flops 7252082688 | bytes 18096128 | tf_op jit(solution)/shard_map/vmap()/dot_general | solution.py:116
  278.6 7.2 %multiply_reduce_fusion.1 = (f32[4,2304]{1,0:T(4,128)S(1)}, f32[4,192,2304]{2,1,0:T(8,128)}, bf16[4,192,2304]{2,1,0:T(8,128)(2,1)}) fusion(f32[4,192,2304]{2,1,0:T(8,128)S(1)} %bitcast.148, f32[4,192,768]{2,1,0:T(8,128)} %fusion.79, f32[4,192,1536]{2,1,0:T(8,128)S(1)} %fusion.4, f32[1,4,192,2304]{3,2,1,0:T(8,128)} %param.12, pred[]{:T(512)} %bitcast.21), kind=kLoop, calls=%fused_computation.27 | loop fusion | flops 14146560 | bytes 31887360 | tf_op jit(solution)/shard_map/vmap()/reduce_sum | solution.py:126
  293.7 13.5 %fusion.51 = f32[4,512,1536]{2,1,0:T(8,128)} fusion(f32[4,192,2304]{2,1,0:T(8,128)S(1)} %bitcast.148, bf16[512,4,192]{0,2,1:T(8,128)(2,1)S(1)} %bitcast.169, f32[4,512]{1,0:T(4,128)S(1)} %rsqrt_bitcast_fusion.5), kind=kOutput, calls=%fused_computation.76 | convolution fusion | flops 7248936960 | bytes 18096128 | tf_op jit(solution)/shard_map/vmap()/dot_general | solution.py:81
  307.1 13.6 %fusion.19 = f32[4,512,192]{1,2,0:T(8,128)} fusion(f32[4,512,1536]{2,1,0:T(8,128)} %fusion.51, f32[4,192,2304]{2,1,0:T(8,128)S(1)} %bitcast.148), kind=kOutput, calls=%fused_computation.31 | convolution fusion | flops 3631742976 | bytes 16515072 | tf_op jit(solution)/shard_map/vmap()/dot_general | solution.py:84
  320.8 16.1 %collective-permute-done = bf16[2048,768]{1,0:T(8,128)(2,1)} collective-permute-done((bf16[2048,768]{1,0:T(8,128)(2,1)S(1)}, bf16[2048,768]{1,0:T(8,128)(2,1)}, u32[]{:S(2)}, u32[]{:S(2)}) %collective-permute-start) | collective-permute-done | bytes 3145760 | tf_op jit(solution)/shard_map/ppermute | solution.py:19
  347.9 8.6 %fusion.60 = f32[4,512,2560]{2,1,0:T(8,128)} fusion(bf16[4,512,192]{1,2,0:T(8,128)(2,1)S(1)} %fusion.103, bf16[4,2048,192]{1,2,0:T(8,128)(2,1)S(1)} %multiply_convert_fusion.1, bf16[512,4,192]{0,2,1:T(8,128)(2,1)S(1)} %bitcast.164, f32[4,512]{1,0:T(4,128)S(1)} %rsqrt_bitcast_fusion.3), kind=kOutput, calls=%fused_computation.85 | convolution fusion | flops 2022309888 | bytes 25698304 | tf_op jit(solution)/shard_map/vmap()/dot_general | solution.py:51
  356.5 22.8 %fusion = (f32[4,512]{1,0:T(4,128)S(1)}, f32[4,512]{1,0:T(4,128)S(1)}, f32[4,512,2560]{2,1,0:T(8,128)}) fusion(f32[2560]{0:T(1024)S(1)} %concatenate.55, pred[512,2560]{1,0:T(8,128)(4,1)} %fusion.44, f32[2560]{0:T(1024)S(1)} %concatenate.60, f32[4,512,2560]{2,1,0:T(8,128)} %fusion.60, bf16[4,512,192]{1,2,0:T(8,128)(2,1)} %fusion.92, ...), kind=kOutput, calls=%fused_computation.2 | convolution fusion | flops 2074734592 | bytes 48017408 | tf_op jit(solution)/shard_map/vmap()/dot_general | solution.py:51
  379.3 11.8 %fusion.108 = bf16[512,4,192]{0,2,1:T(8,128)(2,1)S(1)} fusion(f32[4,512,192]{1,2,0:T(8,128)} %fusion.19, bf16[4,512,192]{1,2,0:T(8,128)(2,1)S(1)} %bitcast.180, bf16[4,2048,192]{1,2,0:T(8,128)(2,1)} %bitcast.171, f32[4,512,2560]{2,1,0:T(8,128)} %get-tuple-element.26, f32[2560]{0:T(1024)S(1)} %concatenate.55, pred[512,2560]{1,0:T(8,128)(4,1)} %fusion.44, ...), kind=kOutput, calls=%fused_computation.135 | convolution fusion | flops 2048917504 | bytes 28592128 | tf_op jit(solution)/shard_map/vmap()/dot_general | solution.py:69
  409.3 70.8 %collective-permute-done.3 = bf16[4,192,2304]{2,1,0:T(8,128)(2,1)} collective-permute-done((bf16[4,192,2304]{2,1,0:T(8,128)(2,1)}, bf16[4,192,2304]{2,1,0:T(8,128)(2,1)}, u32[]{:S(2)}, u32[]{:S(2)}) %collective-permute-start.3) | collective-permute-done | bytes 3538976 | tf_op jit(solution)/shard_map/ppermute | solution.py:19
  484.0 13.3 %fusion.47 = f32[4,512,1536]{2,1,0:T(8,128)} fusion(f32[4,192,2304]{2,1,0:T(8,128)S(1)} %convert_select_fusion, bf16[512,4,192]{0,2,1:T(8,128)(2,1)S(1)} %bitcast.165, f32[4,512]{1,0:T(4,128)S(1)} %rsqrt_bitcast_fusion.3), kind=kOutput, calls=%fused_computation.72 | convolution fusion | flops 7248936960 | bytes 18096128 | tf_op jit(solution)/shard_map/vmap()/dot_general | solution.py:81
  497.3 13.8 %fusion.18 = f32[4,512,192]{1,2,0:T(8,128)} fusion(f32[4,512,1536]{2,1,0:T(8,128)} %fusion.47, f32[4,192,2304]{2,1,0:T(8,128)S(1)} %convert_select_fusion), kind=kOutput, calls=%fused_computation.29 | convolution fusion | flops 3631742976 | bytes 16515072 | tf_op jit(solution)/shard_map/vmap()/dot_general | solution.py:84
  511.1 12.4 %fusion.107 = bf16[512,4,192]{0,2,1:T(8,128)(2,1)} fusion(f32[4,512,192]{1,2,0:T(8,128)} %fusion.18, bf16[4,512,192]{1,2,0:T(8,128)(2,1)S(1)} %bitcast.175, bf16[4,2048,192]{1,2,0:T(8,128)(2,1)} %bitcast.172, f32[4,512,2560]{2,1,0:T(8,128)} %fusion.60, f32[2560]{0:T(1024)S(1)} %concatenate.60, pred[512,2560]{1,0:T(8,128)(4,1)S(1)} %copy-done.10, ...), kind=kOutput, calls=%fused_computation.132 | convolution fusion | flops 2048917504 | bytes 28592128 | tf_op jit(solution)/shard_map/vmap()/dot_general | solution.py:69
  523.5 6.9 %convolution_convert_fusion = bf16[512,3072]{1,0:T(8,128)(2,1)} fusion(bf16[512,768]{0,1:T(8,128)(2,1)} %bitcast.182, bf16[768,3072]{1,0:T(8,128)(2,1)} %param.18), kind=kOutput, calls=%fused_computation.68 | convolution fusion | flops 2417491968 | bytes 8650752 | tf_op jit(solution)/shard_map/dot_general | solution.py:179
  530.4 13.0 %fusion.45 = f32[4,512,1536]{2,1,0:T(8,128)S(1)} fusion(f32[4,192,2304]{2,1,0:T(8,128)} %copy-done.2, bf16[512,4,192]{0,2,1:T(8,128)(2,1)S(1)} %bitcast.157, f32[4,512]{1,0:T(4,128)S(1)} %rsqrt_bitcast_fusion.2), kind=kOutput, calls=%fused_computation.70 | convolution fusion | flops 7248936960 | bytes 18096128 | tf_op jit(solution)/shard_map/vmap()/dot_general | solution.py:93
  543.4 14.4 %add_multiply_fusion = (f32[4,512,768]{2,1,0:T(8,128)S(1)}, f32[4,512,768]{2,1,0:T(8,128)}) fusion(f32[4,512,1536]{2,1,0:T(8,128)S(1)} %fusion.45, f32[4,192,2304]{2,1,0:T(8,128)} %copy-done.2, bf16[4,512,192]{1,2,0:T(8,128)(2,1)S(1)} %bitcast.176, f32[4,512]{1,0:T(4,128)S(1)} %copy-done.14), kind=kOutput, calls=%fused_computation.38 | convolution fusion | flops 3643539456 | bytes 28319744 | tf_op jit(solution)/shard_map/vmap()/dot_general | solution.py:111
  557.9 10.5 %fusion.8 = f32[4,192,1536]{2,1,0:T(8,128)S(1)} fusion(f32[4,512,768]{2,1,0:T(8,128)} %get-tuple-element.8, f32[4,512,768]{2,1,0:T(8,128)S(1)} %get-tuple-element.7, bf16[512,4,192]{0,2,1:T(8,128)(2,1)S(1)} %bitcast.158, f32[4,512]{1,0:T(4,128)S(1)} %rsqrt_bitcast_fusion.2), kind=kOutput, calls=%fused_computation.10 | convolution fusion | flops 7252082688 | bytes 18096128 | tf_op jit(solution)/shard_map/vmap()/dot_general | solution.py:116
  568.3 9.0 %fusion.82 = f32[4,192,768]{2,1,0:T(8,128)S(1)} fusion(f32[4,512,1536]{2,1,0:T(8,128)} %copy-done.6, bf16[4,512,192]{1,2,0:T(8,128)(2,1)S(1)} %bitcast.177, f32[4,512]{1,0:T(4,128)S(1)} %copy-done.14), kind=kOutput, calls=%fused_computation.114 | convolution fusion | flops 3633119232 | bytes 15736832 | tf_op jit(solution)/shard_map/vmap()/dot_general | solution.py:101
  582.0 8.2 %fusion.71 = (f32[1,4,192,2304]{3,2,1,0:T(8,128)}, f32[1,4,192,2304]{3,2,1,0:T(8,128)}) fusion(f32[4,192,768]{2,1,0:T(8,128)S(1)} %fusion.82, f32[4,192,1536]{2,1,0:T(8,128)S(1)} %fusion.8, bf16[4,192,2304]{2,1,0:T(8,128)(2,1)} %collective-permute-done.4, pred[]{:T(512)} %bitcast.48, f32[4,2304]{1,0:T(4,128)S(1)} %add_rsqrt_fusion, ...), kind=kLoop, calls=%fused_computation.97 | loop fusion | flops 17694720 | bytes 31887360 | tf_op jit(solution)/shard_map/broadcast_in_dim | solution.py:255
  (101 shorter events, 93.0 us)
Async XLA Ops:
  7.2 33.3 %copy-start = (bf16[3072,4]{0,1:T(4,128)(2,1)S(1)}, bf16[3072,4]{0,1:T(4,128)(2,1)}, u32[]{:S(2)}) copy-start(bf16[3072,4]{0,1:T(4,128)(2,1)} %param.17) | copy-start | bytes 73732
  7.2 33.2 %all-gather.6.cloned.1.call-start = ((), (), s32[]{:S(2)}) async-start(), calls=%async_computation.5 | async-start | bytes 9437184 | tf_op jit(solution)/shard_map/all_gather | solution.py:198
  7.9 191.3 %all-gather.4.cloned.1.call-start = ((), (), s32[]{:S(2)}) async-start(), calls=%async_computation.2 | async-start | bytes 15040512 | tf_op jit(solution)/shard_map/all_gather | solution.py:202
  8.7 581.6 %reduce-scatter.3.cloned.1.call-start = ((), (), s32[]{:S(2)}) async-start(), calls=%async_computation.3 | async-start | bytes 4718592 | tf_op jit(solution)/shard_map/reduce_scatter | solution.py:180
  10.7 29.7 %collective-permute-start.1 = (bf16[2048]{0:T(1024)(128)(2,1)S(1)}, bf16[2048]{0:T(1024)(128)(2,1)S(1)}, u32[]{:S(2)}, u32[]{:S(2)}) collective-permute-start(bf16[2048]{0:T(1024)(128)(2,1)S(1)} %pad_convert_fusion), channel_id=1, source_target_pairs={{30,0},{0,2},{2,4},{4,6},{6,8},{8,10},{10,12},{12,14},{14,16},{16,... | collective-permute-start | bytes 12296 | tf_op jit(solution)/shard_map/ppermute | solution.py:19
  19.9 6.8 %copy-start.4 = (bf16[4,192,2304]{2,1,0:T(8,128)(2,1)S(1)}, bf16[4,192,2304]{2,1,0:T(8,128)(2,1)}, u32[]{:S(2)}) copy-start(bf16[4,192,2304]{2,1,0:T(8,128)(2,1)} %param.13) | copy-start | bytes 10616836
  24.7 8.9 %slice-start.2 = ((s8[6291456]{0:T(1024)(128)(4,1)}), s8[4194304]{0:T(1024)(128)(4,1)S(1)}, s32[]{:S(2)}) async-start(s8[6291456]{0:T(1024)(128)(4,1)} %bitcast.150), calls=%async_computation.8 | async-start | bytes 8388608
  26.7 6.9 %slice-start.3 = ((s8[6291456]{0:T(1024)(128)(4,1)}), s8[2097152]{0:T(1024)(128)(4,1)S(1)}, s32[]{:S(2)}) async-start(s8[6291456]{0:T(1024)(128)(4,1)} %bitcast.150), calls=%async_computation.9 | async-start | bytes 4194304
  220.5 20.7 %copy-start.12 = (bf16[1,512,768]{1,2,0:T(8,128)(2,1)}, bf16[1,512,768]{1,2,0:T(8,128)(2,1)S(1)}, u32[]{:S(2)}) copy-start(bf16[1,512,768]{1,2,0:T(8,128)(2,1)S(1)} %get-tuple-element.20) | copy-start | bytes 2359300
  262.2 74.7 %collective-permute-start = (bf16[2048,768]{1,0:T(8,128)(2,1)S(1)}, bf16[2048,768]{1,0:T(8,128)(2,1)}, u32[]{:S(2)}, u32[]{:S(2)}) collective-permute-start(bf16[2048,768]{1,0:T(8,128)(2,1)S(1)} %pad_maximum_fusion.1), channel_id=1, source_target_pairs={{30,0},{0,2},{2,4},{4,6},{6,8},{8,10},{10,12},{12,14},{14,16},{16,... | collective-permute-start | bytes 9437192 | tf_op jit(solution)/shard_map/ppermute | solution.py:19
  263.7 14.9 %slice-start = ((s8[7077888]{0:T(1024)(128)(4,1)}), s8[4194304]{0:T(1024)(128)(4,1)S(1)}, s32[]{:S(2)}) async-start(s8[7077888]{0:T(1024)(128)(4,1)} %bitcast.147), calls=%async_computation.6 | async-start | bytes 8388608
  265.6 138.8 %collective-permute-start.2 = (bf16[2048,768]{1,0:T(8,128)(2,1)}, bf16[2048,768]{1,0:T(8,128)(2,1)}, u32[]{:S(2)}, u32[]{:S(2)}) collective-permute-start(bf16[2048,768]{1,0:T(8,128)(2,1)} %pad_maximum_fusion), channel_id=1, source_target_pairs={{30,0},{0,2},{2,4},{4,6},{6,8},{8,10},{10,12},{12,14},{14,16},{16,... | collective-permute-start | bytes 9437192 | tf_op jit(solution)/shard_map/ppermute | solution.py:19
  267.0 11.6 %slice-start.1 = ((s8[7077888]{0:T(1024)(128)(4,1)}), s8[2883584]{0:T(1024)(128)(4,1)S(1)}, s32[]{:S(2)}) async-start(s8[7077888]{0:T(1024)(128)(4,1)} %bitcast.147), calls=%async_computation.7 | async-start | bytes 5767168
  291.2 189.0 %collective-permute-start.3 = (bf16[4,192,2304]{2,1,0:T(8,128)(2,1)}, bf16[4,192,2304]{2,1,0:T(8,128)(2,1)}, u32[]{:S(2)}, u32[]{:S(2)}) collective-permute-start(bf16[4,192,2304]{2,1,0:T(8,128)(2,1)} %multiply_convert_fusion), channel_id=1, source_target_pairs={{30,0},{0,2},{2,4},{4,6},{6,8},{8,10},{10,12},{12,14},{14,16},{16,... | collective-permute-start | bytes 10616840 | tf_op jit(solution)/shard_map/ppermute | solution.py:19
  291.9 285.5 %collective-permute-start.4 = (bf16[4,192,2304]{2,1,0:T(8,128)(2,1)}, bf16[4,192,2304]{2,1,0:T(8,128)(2,1)}, u32[]{:S(2)}, u32[]{:S(2)}) collective-permute-start(bf16[4,192,2304]{2,1,0:T(8,128)(2,1)} %get-tuple-element.11), channel_id=1, source_target_pairs={{30,0},{0,2},{2,4},{4,6},{6,8},{8,10},{10,12},{12,14},{14,16},{16,... | collective-permute-start | bytes 10616840 | tf_op jit(solution)/shard_map/ppermute | solution.py:19
  356.5 22.8 %copy-start.13 = (bf16[1,512,768]{1,2,0:T(8,128)(2,1)S(1)}, bf16[1,512,768]{1,2,0:T(8,128)(2,1)}, u32[]{:S(2)}) copy-start(bf16[1,512,768]{1,2,0:T(8,128)(2,1)} %copy-done.12) | copy-start | bytes 2359300
  397.5 192.8 %reduce-scatter.5.cloned.1.call-start = ((), (), s32[]{:S(2)}) async-start(), calls=%async_computation.4 | async-start | bytes 4718592 | tf_op jit(solution)/shard_map/reduce_scatter | solution.py:180
  484.0 13.3 %copy-start.2 = (f32[4,192,2304]{2,1,0:T(8,128)}, f32[4,192,2304]{2,1,0:T(8,128)S(1)}, u32[]{:S(2)}) copy-start(f32[4,192,2304]{2,1,0:T(8,128)S(1)} %convert_select_fusion) | copy-start | bytes 21233668
  497.3 13.8 %copy-start.10 = (pred[512,2560]{1,0:T(8,128)(4,1)S(1)}, pred[512,2560]{1,0:T(8,128)(4,1)}, u32[]{:S(2)}) copy-start(pred[512,2560]{1,0:T(8,128)(4,1)} %fusion.44) | copy-start | bytes 3932164
  497.3 13.8 %copy-start.11 = (bf16[1,512,768]{1,2,0:T(8,128)(2,1)S(1)}, bf16[1,512,768]{1,2,0:T(8,128)(2,1)}, u32[]{:S(2)}) copy-start(bf16[1,512,768]{1,2,0:T(8,128)(2,1)} %get-tuple-element.17) | copy-start | bytes 2359300
  530.4 13.0 %copy-start.14 = (f32[4,512]{1,0:T(4,128)S(1)}, f32[4,512]{1,0:T(4,128)}, u32[]{:S(2)}) copy-start(f32[4,512]{1,0:T(4,128)} %get-tuple-element.22) | copy-start | bytes 24580
  543.4 14.4 %copy-start.6 = (f32[4,512,1536]{2,1,0:T(8,128)}, f32[4,512,1536]{2,1,0:T(8,128)S(1)}, u32[]{:S(2)}) copy-start(f32[4,512,1536]{2,1,0:T(8,128)S(1)} %fusion.45) | copy-start | bytes 37748740
  568.3 9.0 %copy-start.5 = (bf16[4,192,2304]{2,1,0:T(8,128)(2,1)S(1)}, bf16[4,192,2304]{2,1,0:T(8,128)(2,1)}, u32[]{:S(2)}) copy-start(bf16[4,192,2304]{2,1,0:T(8,128)(2,1)} %param.13) | copy-start | bytes 10616836
  582.0 12.0 %copy-start.1 = (bf16[3072,4]{0,1:T(4,128)(2,1)S(1)}, bf16[3072,4]{0,1:T(4,128)(2,1)}, u32[]{:S(2)}) copy-start(bf16[3072,4]{0,1:T(4,128)(2,1)} %param.17) | copy-start | bytes 73732
  (4 other events, 16.0 us)
Sparse Core Ops, SparseCore 0:
  9.5 19.4 all-gather.5
  31.7 167.4 all-gather.3
  397.6 6.8 reduce-scatter.2
  530.5 6.8 reduce-scatter.4
where the time goes:
time: 610 us; the launch traced here: 601 us
  waiting for transfers between devices  248 us (41%)
  matrix products  240 us (39%)
  other arithmetic  60.5 us (10%)
  local copies, waits for them, and re-layouts  27.6 us (5%)
  between operations  17.2 us (3%)
  starting transfers between devices  7.44 us (1%)
    all_gather x1, waiting for transfers between devices, body(): lax.all_gather(qkv_weight, 'seq', axis=1, tiled=True)  153 us
    ppermute x5, waiting for transfers between devices, passed_along(): return lax.ppermute(block, axis, route)  93.7 us
    dot_general x2, matrix products, head_span(): lax.dot_general(query_unit.astype(jnp.bfloat16), context_keys, (((1,), (1...  31.4 us
    dot_general x2, matrix products, head_span(): jnp.dot(out_grad, down_proj, precision=highest, preferred_element_type=jn...  28 us
    dot_general x2, matrix products, head_span(): lax.dot_general(mixed_hidden, down_proj, (((1,), (1,)), ((), ())), precis...  27.4 us
    dot_general x2, matrix products, head_span(): jnp.dot(query_in, up_proj, precision=highest, preferred_element_type=jnp....  26.7 us
    dot_general x2, matrix products, head_span(): jnp.dot(key_in, up_proj, precision=highest, preferred_element_type=jnp.fl...  26.2 us
    dot_general x2, matrix products, head_span(): jnp.dot(soft_weights.astype(jnp.bfloat16), context_values, preferred_elem...  24.2 us
  transfers between devices with their start and end apart: 9, of which 4 were waited for; matrix products, arithmetic and copies ran while one was open for 43% of the time, Pallas kernels for 0%

commit v1 on v0

--- a/solution.py
+++ b/solution.py
@@ -196,11 +196,14 @@
 ):
     position_index = lax.axis_index("seq")
     features = lax.all_gather(tokens[0], "head", axis=1, tiled=True)
+
+    def sites_check(frame, comm_axis):
+        built = lax.all_gather(frame, comm_axis)
+        all_values = jnp.concatenate(built, 1)
+        return all_values
+
     projected = jnp.einsum(
-        "tr,crh->cth",
-        features,
-        lax.all_gather(qkv_weight, "seq", axis=1, tiled=True),
-        preferred_element_type=jnp.float32,
+        "tr,crh->cth", features, sites_check(qkv_weight, "seq"), preferred_element_type=jnp.float32
     )
     projected_bf = projected.astype(jnp.bfloat16)
     step_sizes = (

time: 610 us -> 626 us (1.026)
  local copies, waits for them, and re-layouts: 27.6 us -> 40.4 us
    reshape x0 -> x1, local copies, waits for them, and re-layouts: none -> 12.7 us  [sites_check(): all_values = jnp.concatenate(built, 1)]
  transfers between devices with their start and end apart: 9 -> 9, of which waited for: 4 -> 4; matrix products, arithmetic and copies ran while one was open for 43% -> 42% of each run, Pallas kernels for 0% -> 0%
where the time goes in v1:
time: 626 us; the launch traced here: 618 us
  waiting for transfers between devices  248 us (40%)
  matrix products  244 us (39%)
  other arithmetic  60.5 us (10%)
  local copies, waits for them, and re-layouts  40.4 us (6%)
  between operations  17.2 us (3%)
  starting transfers between devices  7.57 us (1%)
    all_gather x1, waiting for transfers between devices, sites_check(): built = lax.all_gather(frame, comm_axis)  153 us
    ppermute x5, waiting for transfers between devices, passed_along(): return lax.ppermute(block, axis, route)  93.8 us
    dot_general x2, matrix products, head_span(): lax.dot_general(query_unit.astype(jnp.bfloat16), context_keys, (((1,), (1...  31.4 us
    dot_general x2, matrix products, head_span(): jnp.dot(out_grad, down_proj, precision=highest, preferred_element_type=jn...  28.5 us
    dot_general x2, matrix products, head_span(): lax.dot_general(mixed_hidden, down_proj, (((1,), (1,)), ((), ())), precis...  27.4 us
    dot_general x2, matrix products, head_span(): jnp.dot(query_in, up_proj, precision=highest, preferred_element_type=jnp....  26.4 us
    dot_general x2, matrix products, head_span(): jnp.dot(key_in, up_proj, precision=highest, preferred_element_type=jnp.fl...  26.4 us
    dot_general x2, matrix products, head_span(): jnp.dot(soft_weights.astype(jnp.bfloat16), context_values, preferred_elem...  24.2 us
  transfers between devices with their start and end apart: 9, of which 4 were waited for; matrix products, arithmetic and copies ran while one was open for 42% of the time, Pallas kernels for 0%

profile of v1, /device:TPU:0, one launch (start us, length us, event | category | flops | bytes accessed | tf_op | source)
XLA Modules:
  0.0 617.6 jit_solution(3801463665782910838)
XLA Ops:
  46.4 152.9 %all-gather.5.cloned.1.call-done = bf16[48,192,768]{2,1,0:T(8,128)(2,1)} async-done(((bf16[3,192,768]{2,1,0:T(8,128)(2,1)}), bf16[48,192,768]{2,1,0:T(8,128)(2,1)}) %all-gather.5.cloned.1.call-update) | async-done | bytes 14155792 | tf_op jit(solution)/shard_map/all_gather | solution.py:201
  199.3 12.7 %copy.35 = bf16[3,16,192,768]{3,2,1,0:T(8,128)(2,1)} copy(bf16[3,16,192,768]{3,2,0,1:T(8,128)(2,1)} %bitcast.172) | data formatting | bytes 28311552 | tf_op jit(solution)/shard_map/reshape | solution.py:202
  212.0 18.0 %convert_bitcast_fusion = bf16[3,1024,768]{1,2,0:T(8,128)(2,1)S(1)} fusion(bf16[3,3072,768]{2,1,0:T(8,128)(2,1)} %bitcast.173, bf16[1,1024,3072]{2,1,0:T(8,128)(2,1)S(1)} %bitcast.180), kind=kOutput, calls=%fused_computation.67 | convolution fusion | flops 14497873920 | bytes 25165824 | tf_op jit(solution)/shard_map/tr,crh->cth/dot_general | solution.py:205
  232.1 13.4 %fusion.49 = f32[4,512,1536]{2,1,0:T(8,128)} fusion(f32[4,192,2304]{2,1,0:T(8,128)S(1)} %bitcast.152, bf16[512,4,192]{0,2,1:T(8,128)(2,1)S(1)} %bitcast.166, f32[4,512]{1,0:T(4,128)S(1)} %rsqrt_bitcast_fusion.4), kind=kOutput, calls=%fused_computation.74 | convolution fusion | flops 7248936960 | bytes 18096128 | tf_op jit(solution)/shard_map/vmap()/dot_general | solution.py:93
  245.5 11.8 %fusion.79 = f32[4,192,768]{2,1,0:T(8,128)} fusion(f32[4,512,1536]{2,1,0:T(8,128)} %fusion.49, bf16[4,512,192]{1,2,0:T(8,128)(2,1)S(1)} %bitcast.188, f32[4,512]{1,0:T(4,128)S(1)} %get-tuple-element.23), kind=kOutput, calls=%fused_computation.113 | convolution fusion | flops 3633119232 | bytes 15736832 | tf_op jit(solution)/shard_map/vmap()/dot_general | solution.py:101
  257.3 14.0 %add_multiply_fusion.1 = (f32[4,512,768]{2,1,0:T(8,128)}, f32[4,512,768]{2,1,0:T(8,128)}) fusion(f32[4,512,1536]{2,1,0:T(8,128)} %fusion.49, f32[4,192,2304]{2,1,0:T(8,128)S(1)} %bitcast.152, bf16[4,512,192]{1,2,0:T(8,128)(2,1)S(1)} %bitcast.189, f32[4,512]{1,0:T(4,128)S(1)} %get-tuple-element.23), kind=kOutput, calls=%fused_computation.49 | convolution fusion | flops 3643539456 | bytes 28319744 | tf_op jit(solution)/shard_map/vmap()/dot_general | solution.py:111
  283.6 11.5 %fusion.4 = f32[4,192,1536]{2,1,0:T(8,128)S(1)} fusion(f32[4,512,768]{2,1,0:T(8,128)} %get-tuple-element.10, f32[4,512,768]{2,1,0:T(8,128)} %get-tuple-element.9, bf16[512,4,192]{0,2,1:T(8,128)(2,1)S(1)} %bitcast.167, f32[4,512]{1,0:T(4,128)S(1)} %rsqrt_bitcast_fusion.4), kind=kOutput, calls=%fused_computation.6 | convolution fusion | flops 7252082688 | bytes 18096128 | tf_op jit(solution)/shard_map/vmap()/dot_general | solution.py:116
  295.2 7.2 %multiply_reduce_fusion.1 = (f32[4,2304]{1,0:T(4,128)S(1)}, f32[4,192,2304]{2,1,0:T(8,128)}, bf16[4,192,2304]{2,1,0:T(8,128)(2,1)}) fusion(f32[4,192,2304]{2,1,0:T(8,128)S(1)} %bitcast.154, f32[4,192,768]{2,1,0:T(8,128)} %fusion.79, f32[4,192,1536]{2,1,0:T(8,128)S(1)} %fusion.4, f32[1,4,192,2304]{3,2,1,0:T(8,128)} %param.12, pred[]{:T(512)} %bitcast.24), kind=kLoop, calls=%fused_computation.27 | loop fusion | flops 14146560 | bytes 31887360 | tf_op jit(solution)/shard_map/vmap()/reduce_sum | solution.py:126
  310.4 13.2 %fusion.51 = f32[4,512,1536]{2,1,0:T(8,128)} fusion(f32[4,192,2304]{2,1,0:T(8,128)S(1)} %bitcast.154, bf16[512,4,192]{0,2,1:T(8,128)(2,1)S(1)} %bitcast.177, f32[4,512]{1,0:T(4,128)S(1)} %rsqrt_bitcast_fusion.5), kind=kOutput, calls=%fused_computation.76 | convolution fusion | flops 7248936960 | bytes 18096128 | tf_op jit(solution)/shard_map/vmap()/dot_general | solution.py:81
  323.6 13.7 %fusion.19 = f32[4,512,192]{1,2,0:T(8,128)} fusion(f32[4,512,1536]{2,1,0:T(8,128)} %fusion.51, f32[4,192,2304]{2,1,0:T(8,128)S(1)} %bitcast.154), kind=kOutput, calls=%fused_computation.31 | convolution fusion | flops 3631742976 | bytes 16515072 | tf_op jit(solution)/shard_map/vmap()/dot_general | solution.py:84
  337.3 16.2 %collective-permute-done = bf16[2048,768]{1,0:T(8,128)(2,1)} collective-permute-done((bf16[2048,768]{1,0:T(8,128)(2,1)S(1)}, bf16[2048,768]{1,0:T(8,128)(2,1)}, u32[]{:S(2)}, u32[]{:S(2)}) %collective-permute-start) | collective-permute-done | bytes 3145760 | tf_op jit(solution)/shard_map/ppermute | solution.py:19
  364.5 8.6 %fusion.60 = f32[4,512,2560]{2,1,0:T(8,128)} fusion(bf16[4,512,192]{1,2,0:T(8,128)(2,1)S(1)} %fusion.103, bf16[4,2048,192]{1,2,0:T(8,128)(2,1)S(1)} %multiply_convert_fusion.1, bf16[512,4,192]{0,2,1:T(8,128)(2,1)S(1)} %bitcast.170, f32[4,512]{1,0:T(4,128)S(1)} %rsqrt_bitcast_fusion.3), kind=kOutput, calls=%fused_computation.85 | convolution fusion | flops 2022309888 | bytes 25698304 | tf_op jit(solution)/shard_map/vmap()/dot_general | solution.py:51
  373.1 22.8 %fusion = (f32[4,512]{1,0:T(4,128)S(1)}, f32[4,512]{1,0:T(4,128)S(1)}, f32[4,512,2560]{2,1,0:T(8,128)}) fusion(f32[2560]{0:T(1024)S(1)} %concatenate.55, pred[512,2560]{1,0:T(8,128)(4,1)} %fusion.44, f32[2560]{0:T(1024)S(1)} %concatenate.60, f32[4,512,2560]{2,1,0:T(8,128)} %fusion.60, bf16[4,512,192]{1,2,0:T(8,128)(2,1)} %fusion.92, ...), kind=kOutput, calls=%fused_computation.2 | convolution fusion | flops 2074734592 | bytes 48017408 | tf_op jit(solution)/shard_map/vmap()/dot_general | solution.py:51
  395.9 11.8 %fusion.108 = bf16[512,4,192]{0,2,1:T(8,128)(2,1)S(1)} fusion(f32[4,512,192]{1,2,0:T(8,128)} %fusion.19, bf16[4,512,192]{1,2,0:T(8,128)(2,1)S(1)} %bitcast.190, bf16[4,2048,192]{1,2,0:T(8,128)(2,1)} %bitcast.181, f32[4,512,2560]{2,1,0:T(8,128)} %get-tuple-element.26, f32[2560]{0:T(1024)S(1)} %concatenate.55, pred[512,2560]{1,0:T(8,128)(4,1)} %fusion.44, ...), kind=kOutput, calls=%fused_computation.135 | convolution fusion | flops 2048917504 | bytes 28592128 | tf_op jit(solution)/shard_map/vmap()/dot_general | solution.py:69
  425.9 70.8 %collective-permute-done.3 = bf16[4,192,2304]{2,1,0:T(8,128)(2,1)} collective-permute-done((bf16[4,192,2304]{2,1,0:T(8,128)(2,1)}, bf16[4,192,2304]{2,1,0:T(8,128)(2,1)}, u32[]{:S(2)}, u32[]{:S(2)}) %collective-permute-start.3) | collective-permute-done | bytes 3538976 | tf_op jit(solution)/shard_map/ppermute | solution.py:19
  500.6 13.2 %fusion.47 = f32[4,512,1536]{2,1,0:T(8,128)} fusion(f32[4,192,2304]{2,1,0:T(8,128)S(1)} %convert_select_fusion, bf16[512,4,192]{0,2,1:T(8,128)(2,1)S(1)} %bitcast.171, f32[4,512]{1,0:T(4,128)S(1)} %rsqrt_bitcast_fusion.3), kind=kOutput, calls=%fused_computation.72 | convolution fusion | flops 7248936960 | bytes 18096128 | tf_op jit(solution)/shard_map/vmap()/dot_general | solution.py:81
  513.8 13.8 %fusion.18 = f32[4,512,192]{1,2,0:T(8,128)} fusion(f32[4,512,1536]{2,1,0:T(8,128)} %fusion.47, f32[4,192,2304]{2,1,0:T(8,128)S(1)} %convert_select_fusion), kind=kOutput, calls=%fused_computation.29 | convolution fusion | flops 3631742976 | bytes 16515072 | tf_op jit(solution)/shard_map/vmap()/dot_general | solution.py:84
  527.6 12.5 %fusion.107 = bf16[512,4,192]{0,2,1:T(8,128)(2,1)} fusion(f32[4,512,192]{1,2,0:T(8,128)} %fusion.18, bf16[4,512,192]{1,2,0:T(8,128)(2,1)S(1)} %bitcast.185, bf16[4,2048,192]{1,2,0:T(8,128)(2,1)} %bitcast.182, f32[4,512,2560]{2,1,0:T(8,128)} %fusion.60, f32[2560]{0:T(1024)S(1)} %concatenate.60, pred[512,2560]{1,0:T(8,128)(4,1)S(1)} %copy-done.10, ...), kind=kOutput, calls=%fused_computation.132 | convolution fusion | flops 2048917504 | bytes 28592128 | tf_op jit(solution)/shard_map/vmap()/dot_general | solution.py:69
  540.1 6.9 %convolution_convert_fusion = bf16[512,3072]{1,0:T(8,128)(2,1)} fusion(bf16[512,768]{0,1:T(8,128)(2,1)} %bitcast.192, bf16[768,3072]{1,0:T(8,128)(2,1)} %param.18), kind=kOutput, calls=%fused_computation.68 | convolution fusion | flops 2417491968 | bytes 8650752 | tf_op jit(solution)/shard_map/dot_general | solution.py:179
  547.0 13.0 %fusion.45 = f32[4,512,1536]{2,1,0:T(8,128)S(1)} fusion(f32[4,192,2304]{2,1,0:T(8,128)} %copy-done.2, bf16[512,4,192]{0,2,1:T(8,128)(2,1)S(1)} %bitcast.163, f32[4,512]{1,0:T(4,128)S(1)} %rsqrt_bitcast_fusion.2), kind=kOutput, calls=%fused_computation.70 | convolution fusion | flops 7248936960 | bytes 18096128 | tf_op jit(solution)/shard_map/vmap()/dot_general | solution.py:93
  560.0 14.4 %add_multiply_fusion = (f32[4,512,768]{2,1,0:T(8,128)S(1)}, f32[4,512,768]{2,1,0:T(8,128)}) fusion(f32[4,512,1536]{2,1,0:T(8,128)S(1)} %fusion.45, f32[4,192,2304]{2,1,0:T(8,128)} %copy-done.2, bf16[4,512,192]{1,2,0:T(8,128)(2,1)S(1)} %bitcast.186, f32[4,512]{1,0:T(4,128)S(1)} %copy-done.14), kind=kOutput, calls=%fused_computation.38 | convolution fusion | flops 3643539456 | bytes 28319744 | tf_op jit(solution)/shard_map/vmap()/dot_general | solution.py:111
  574.4 10.5 %fusion.8 = f32[4,192,1536]{2,1,0:T(8,128)S(1)} fusion(f32[4,512,768]{2,1,0:T(8,128)} %get-tuple-element.8, f32[4,512,768]{2,1,0:T(8,128)S(1)} %get-tuple-element.7, bf16[512,4,192]{0,2,1:T(8,128)(2,1)S(1)} %bitcast.164, f32[4,512]{1,0:T(4,128)S(1)} %rsqrt_bitcast_fusion.2), kind=kOutput, calls=%fused_computation.10 | convolution fusion | flops 7252082688 | bytes 18096128 | tf_op jit(solution)/shard_map/vmap()/dot_general | solution.py:116
  584.9 9.0 %fusion.82 = f32[4,192,768]{2,1,0:T(8,128)S(1)} fusion(f32[4,512,1536]{2,1,0:T(8,128)} %copy-done.6, bf16[4,512,192]{1,2,0:T(8,128)(2,1)S(1)} %bitcast.187, f32[4,512]{1,0:T(4,128)S(1)} %copy-done.14), kind=kOutput, calls=%fused_computation.114 | convolution fusion | flops 3633119232 | bytes 15736832 | tf_op jit(solution)/shard_map/vmap()/dot_general | solution.py:101
  598.6 8.2 %fusion.71 = (f32[1,4,192,2304]{3,2,1,0:T(8,128)}, f32[1,4,192,2304]{3,2,1,0:T(8,128)}) fusion(f32[4,192,768]{2,1,0:T(8,128)S(1)} %fusion.82, f32[4,192,1536]{2,1,0:T(8,128)S(1)} %fusion.8, bf16[4,192,2304]{2,1,0:T(8,128)(2,1)} %collective-permute-done.4, pred[]{:T(512)} %bitcast.51, f32[4,2304]{1,0:T(4,128)S(1)} %add_rsqrt_fusion, ...), kind=kLoop, calls=%fused_computation.97 | loop fusion | flops 17694720 | bytes 31887360 | tf_op jit(solution)/shard_map/broadcast_in_dim | solution.py:258
  (112 shorter events, 100.2 us)
Async XLA Ops:
  7.2 33.3 %copy-start = (bf16[3072,4]{0,1:T(4,128)(2,1)S(1)}, bf16[3072,4]{0,1:T(4,128)(2,1)}, u32[]{:S(2)}) copy-start(bf16[3072,4]{0,1:T(4,128)(2,1)} %param.17) | copy-start | bytes 73732
  7.2 33.3 %all-gather.7.cloned.1.call-start = ((), (), s32[]{:S(2)}) async-start(), calls=%async_computation.5 | async-start | bytes 9437184 | tf_op jit(solution)/shard_map/all_gather | solution.py:198
  7.9 191.4 %all-gather.5.cloned.1.call-start = ((), (), s32[]{:S(2)}) async-start(), calls=%async_computation.4 | async-start | bytes 15040512 | tf_op jit(solution)/shard_map/all_gather | solution.py:201
  8.7 598.2 %reduce-scatter.3.cloned.1.call-start = ((), (), s32[]{:S(2)}) async-start(), calls=%async_computation.2 | async-start | bytes 4718592 | tf_op jit(solution)/shard_map/reduce_scatter | solution.py:180
  10.7 29.7 %collective-permute-start.1 = (bf16[2048]{0:T(1024)(128)(2,1)S(1)}, bf16[2048]{0:T(1024)(128)(2,1)S(1)}, u32[]{:S(2)}, u32[]{:S(2)}) collective-permute-start(bf16[2048]{0:T(1024)(128)(2,1)S(1)} %pad_convert_fusion), channel_id=1, source_target_pairs={{30,0},{0,2},{2,4},{4,6},{6,8},{8,10},{10,12},{12,14},{14,16},{16,... | collective-permute-start | bytes 12296 | tf_op jit(solution)/shard_map/ppermute | solution.py:19
  40.5 171.5 %slice-start.6 = ((s8[6291456]{0:T(1024)(128)(4,1)}), s8[2097152]{0:T(1024)(128)(4,1)S(1)}, s32[]{:S(2)}) async-start(s8[6291456]{0:T(1024)(128)(4,1)} %bitcast.179), calls=%async_computation.12 | async-start | bytes 4194304
  199.3 12.7 %slice-start.7 = ((s8[6291456]{0:T(1024)(128)(4,1)}), s8[4194304]{0:T(1024)(128)(4,1)S(1)}, s32[]{:S(2)}) async-start(s8[6291456]{0:T(1024)(128)(4,1)} %bitcast.179), calls=%async_computation.13 | async-start | bytes 8388608
  199.3 32.7 %slice-start = ((s8[7077888]{0:T(1024)(128)(4,1)}), s8[4194304]{0:T(1024)(128)(4,1)S(1)}, s32[]{:S(2)}) async-start(s8[7077888]{0:T(1024)(128)(4,1)} %bitcast.151), calls=%async_computation.6 | async-start | bytes 8388608
  212.0 20.0 %slice-start.1 = ((s8[7077888]{0:T(1024)(128)(4,1)}), s8[2883584]{0:T(1024)(128)(4,1)S(1)}, s32[]{:S(2)}) async-start(s8[7077888]{0:T(1024)(128)(4,1)} %bitcast.151), calls=%async_computation.7 | async-start | bytes 5767168
  231.8 25.5 %copy-start.12 = (bf16[1,512,768]{1,2,0:T(8,128)(2,1)}, bf16[1,512,768]{1,2,0:T(8,128)(2,1)S(1)}, u32[]{:S(2)}) copy-start(bf16[1,512,768]{1,2,0:T(8,128)(2,1)S(1)} %get-tuple-element.20) | copy-start | bytes 2359300
  278.7 74.7 %collective-permute-start = (bf16[2048,768]{1,0:T(8,128)(2,1)S(1)}, bf16[2048,768]{1,0:T(8,128)(2,1)}, u32[]{:S(2)}, u32[]{:S(2)}) collective-permute-start(bf16[2048,768]{1,0:T(8,128)(2,1)S(1)} %pad_maximum_fusion.1), channel_id=1, source_target_pairs={{30,0},{0,2},{2,4},{4,6},{6,8},{8,10},{10,12},{12,14},{14,16},{16,... | collective-permute-start | bytes 9437192 | tf_op jit(solution)/shard_map/ppermute | solution.py:19
  280.2 14.9 %slice-start.2 = ((s8[7077888]{0:T(1024)(128)(4,1)}), s8[4194304]{0:T(1024)(128)(4,1)S(1)}, s32[]{:S(2)}) async-start(s8[7077888]{0:T(1024)(128)(4,1)} %bitcast.153), calls=%async_computation.8 | async-start | bytes 8388608
  282.1 138.8 %collective-permute-start.2 = (bf16[2048,768]{1,0:T(8,128)(2,1)}, bf16[2048,768]{1,0:T(8,128)(2,1)}, u32[]{:S(2)}, u32[]{:S(2)}) collective-permute-start(bf16[2048,768]{1,0:T(8,128)(2,1)} %pad_maximum_fusion), channel_id=1, source_target_pairs={{30,0},{0,2},{2,4},{4,6},{6,8},{8,10},{10,12},{12,14},{14,16},{16,... | collective-permute-start | bytes 9437192 | tf_op jit(solution)/shard_map/ppermute | solution.py:19
  283.6 11.6 %slice-start.3 = ((s8[7077888]{0:T(1024)(128)(4,1)}), s8[2883584]{0:T(1024)(128)(4,1)S(1)}, s32[]{:S(2)}) async-start(s8[7077888]{0:T(1024)(128)(4,1)} %bitcast.153), calls=%async_computation.9 | async-start | bytes 5767168
  307.7 189.0 %collective-permute-start.3 = (bf16[4,192,2304]{2,1,0:T(8,128)(2,1)}, bf16[4,192,2304]{2,1,0:T(8,128)(2,1)}, u32[]{:S(2)}, u32[]{:S(2)}) collective-permute-start(bf16[4,192,2304]{2,1,0:T(8,128)(2,1)} %multiply_convert_fusion), channel_id=1, source_target_pairs={{30,0},{0,2},{2,4},{4,6},{6,8},{8,10},{10,12},{12,14},{14,16},{16,... | collective-permute-start | bytes 10616840 | tf_op jit(solution)/shard_map/ppermute | solution.py:19
  308.4 285.5 %collective-permute-start.4 = (bf16[4,192,2304]{2,1,0:T(8,128)(2,1)}, bf16[4,192,2304]{2,1,0:T(8,128)(2,1)}, u32[]{:S(2)}, u32[]{:S(2)}) collective-permute-start(bf16[4,192,2304]{2,1,0:T(8,128)(2,1)} %get-tuple-element.11), channel_id=1, source_target_pairs={{30,0},{0,2},{2,4},{4,6},{6,8},{8,10},{10,12},{12,14},{14,16},{16,... | collective-permute-start | bytes 10616840 | tf_op jit(solution)/shard_map/ppermute | solution.py:19
  373.1 22.8 %copy-start.13 = (bf16[1,512,768]{1,2,0:T(8,128)(2,1)S(1)}, bf16[1,512,768]{1,2,0:T(8,128)(2,1)}, u32[]{:S(2)}) copy-start(bf16[1,512,768]{1,2,0:T(8,128)(2,1)} %copy-done.12) | copy-start | bytes 2359300
  414.1 192.8 %reduce-scatter.5.cloned.1.call-start = ((), (), s32[]{:S(2)}) async-start(), calls=%async_computation.3 | async-start | bytes 4718592 | tf_op jit(solution)/shard_map/reduce_scatter | solution.py:180
  500.6 13.2 %copy-start.2 = (f32[4,192,2304]{2,1,0:T(8,128)}, f32[4,192,2304]{2,1,0:T(8,128)S(1)}, u32[]{:S(2)}) copy-start(f32[4,192,2304]{2,1,0:T(8,128)S(1)} %convert_select_fusion) | copy-start | bytes 21233668
  513.8 13.8 %copy-start.10 = (pred[512,2560]{1,0:T(8,128)(4,1)S(1)}, pred[512,2560]{1,0:T(8,128)(4,1)}, u32[]{:S(2)}) copy-start(pred[512,2560]{1,0:T(8,128)(4,1)} %fusion.44) | copy-start | bytes 3932164
  513.8 13.8 %copy-start.11 = (bf16[1,512,768]{1,2,0:T(8,128)(2,1)S(1)}, bf16[1,512,768]{1,2,0:T(8,128)(2,1)}, u32[]{:S(2)}) copy-start(bf16[1,512,768]{1,2,0:T(8,128)(2,1)} %get-tuple-element.17) | copy-start | bytes 2359300
  547.0 13.0 %copy-start.14 = (f32[4,512]{1,0:T(4,128)S(1)}, f32[4,512]{1,0:T(4,128)}, u32[]{:S(2)}) copy-start(f32[4,512]{1,0:T(4,128)} %get-tuple-element.22) | copy-start | bytes 24580
  560.0 14.4 %copy-start.6 = (f32[4,512,1536]{2,1,0:T(8,128)}, f32[4,512,1536]{2,1,0:T(8,128)S(1)}, u32[]{:S(2)}) copy-start(f32[4,512,1536]{2,1,0:T(8,128)S(1)} %fusion.45) | copy-start | bytes 37748740
  598.6 12.0 %copy-start.1 = (bf16[3072,4]{0,1:T(4,128)(2,1)S(1)}, bf16[3072,4]{0,1:T(4,128)(2,1)}, u32[]{:S(2)}) copy-start(bf16[3072,4]{0,1:T(4,128)(2,1)} %param.17) | copy-start | bytes 73732
  (8 other events, 47.6 us)
Sparse Core Ops, SparseCore 0:
  9.5 19.4 all-gather.6
  31.8 167.4 all-gather.4
  414.2 6.8 reduce-scatter.2
  547.1 6.8 reduce-scatter.4
